TPU v7x, 32 devices: a whole 2x2x4 slice. The times are simulated.
32 devices in a mesh: row: 2 (over x), col: 8 (over z, y), layer: 2 (over core).
Axes of the slice: x: 2, y: 2, z: 4, core: 2. Of those that a mesh axis runs over, the one named last changes fastest.
Arguments:
- owned_blocks: bfloat16 [512, 32, 128, 128], P(('row', 'col', 'layer')), may hold values from -1 to 1
- slot_rows: int32 [512], P(('row', 'col', 'layer')), may hold values from -1 to 255, as said below
- block_cols: int32 [512, 32], P(('row', 'col', 'layer')), may hold values from 0 to 255, as said below
Outputs:
- product_blocks: bfloat16 [256, 32, 128, 128], P(('row', 'layer'), 'col')
Inputs may be any that keep to these rules, and one draw needn't show every extreme that they name: `slot_rows`: every block row appears in exactly one slot. The 16 slots of the device at grid row r, grid column c and layer l (slots ((r * 8 + c) * 2 + l) * 16 onward) hold only block rows i with i // 128 = r and (i // 16) % 2 = l, or -1. In every grid row and layer some device uses all of its slots. block_cols[s, p] lies in panel p, between p * 8 and p * 8 + 7, also for unused slots.
All inputs are finite; a program needn't handle non-finite values.
Results may differ from a plain program's by a relative error of at most 0.001.
Values may be sent and summed in bfloat16 or wider, within the bound.
A program may use at most 256 MiB of HBM per device.

v0:
```python
import jax
import jax.numpy as jnp
from jax import lax
from jax.sharding import PartitionSpec as P

NB = 256


def grid_positions(row_ids, panels, panel_width, grid_row, rows_grid, layers, per_device):
    panel_index = row_ids // panel_width
    offset = row_ids % panel_width
    local_panel = panel_index - grid_row * (panels // rows_grid)
    layer_of = panel_index // per_device % layers
    half_rows = panels // rows_grid * panel_width // layers
    within = (
        local_panel // (per_device * layers) * per_device + local_panel % per_device
    ) * panel_width + offset
    placed = layer_of * half_rows + within
    return jnp.where(row_ids >= 0, placed, layers * half_rows).astype(jnp.int32)


def shards(owned_blocks, slot_rows, block_cols):
    own_slots = owned_blocks.shape[0]
    panels = owned_blocks.shape[1]
    block_size = owned_blocks.shape[2]
    rows_grid = lax.axis_size("row")
    cols_grid = lax.axis_size("col")
    layers = lax.axis_size("layer")
    per_device = panels // (cols_grid * layers)
    panel_width = NB // panels
    tile_rows = NB // rows_grid
    slots_here = layers * per_device
    outgoing = (
        owned_blocks.reshape(own_slots, cols_grid * layers, per_device, block_size, block_size),
        block_cols.reshape(own_slots, cols_grid * layers, per_device),
        jnp.broadcast_to(slot_rows[:, None], (own_slots, cols_grid * layers)),
        jnp.broadcast_to(block_cols[:, None, :], (own_slots, cols_grid * layers, panels)),
    )
    got_blocks, got_cols, got_rows, got_every = (
        lax.all_to_all(outgoing[0], ("col", "layer"), split_axis=1, concat_axis=0, tiled=True),
        lax.all_to_all(outgoing[1], ("col", "layer"), split_axis=1, concat_axis=0, tiled=True),
        lax.all_to_all(outgoing[2], ("col", "layer"), split_axis=1, concat_axis=0, tiled=True),
        lax.all_to_all(outgoing[3], ("col", "layer"), split_axis=1, concat_axis=0, tiled=True),
    )
    got_rows = got_rows.reshape(-1)
    slot_total = got_rows.shape[0]
    got_blocks = got_blocks.reshape(slot_total, per_device, block_size, block_size)
    got_cols = got_cols.reshape(slot_total, per_device)
    got_every = got_every.reshape(slot_total, panels)
    target = grid_positions(
        got_rows, panels, panel_width, lax.axis_index("row"), rows_grid, layers, per_device
    )
    row_tile = (
        jnp.zeros((tile_rows, per_device, block_size, block_size), jnp.bfloat16)
        .at[target]
        .set(got_blocks, mode="drop")
    )
    col_tile = jnp.zeros((tile_rows, per_device), jnp.int32).at[target].set(got_cols, mode="drop")
    every_cols = jnp.zeros((tile_rows, panels), jnp.int32).at[target].set(got_every, mode="drop")
    target_cols = lax.dynamic_slice_in_dim(
        every_cols, lax.axis_index("col") * slots_here, slots_here, 1
    )
    column_tile, column_ids = (
        lax.all_to_all(row_tile, "layer", split_axis=0, concat_axis=1, tiled=True),
        lax.all_to_all(col_tile, "layer", split_axis=0, concat_axis=1, tiled=True),
    )
    column_table, column_ids = (
        lax.all_gather(column_tile, "row", axis=0, tiled=True),
        lax.all_gather(column_ids, "row", axis=0, tiled=True),
    )
    column_table = column_table.reshape(
        panels // layers, panel_width, slots_here, block_size, block_size
    )
    column_ids = column_ids.reshape(panels // layers, panel_width, slots_here)
    initial = jnp.zeros((tile_rows, slots_here, block_size, block_size), jnp.float32)
    piece_blocks = lax.all_gather(row_tile, "col", axis=1, tiled=True)
    piece_cols = lax.all_gather(col_tile, "col", axis=1, tiled=True)
    panel_count = piece_blocks.shape[1]
    panel_steps = jnp.arange(panel_count, dtype=jnp.int32)
    offsets = piece_cols % panel_width

    def one_block(block_index):
        left_blocks = lax.dynamic_slice_in_dim(piece_blocks, block_index * 8, 8, 0)
        row_offsets = lax.dynamic_slice_in_dim(offsets, block_index * 8, 8, 0)
        wanted = lax.dynamic_slice_in_dim(target_cols, block_index * 8, 8, 0)
        chosen = column_table[panel_steps[None, :], row_offsets]
        chosen_ids = column_ids[panel_steps[None, :], row_offsets]
        matched = chosen_ids == wanted[:, None, :]
        chosen = jnp.where(matched[:, :, :, None, None], chosen, jnp.zeros((), jnp.bfloat16))
        return jnp.einsum(
            "mtab,mtsbc->msac", left_blocks, chosen, preferred_element_type=jnp.float32
        )

    products = lax.map(one_block, jnp.arange(tile_rows // 8, dtype=jnp.int32))
    partial_value = initial + products.reshape(initial.shape)
    own_rows = lax.psum_scatter(partial_value, "layer", scatter_dimension=0, tiled=True)
    return own_rows.astype(jnp.bfloat16)


def solution(mesh):
    return jax.shard_map(
        shards,
        mesh=mesh,
        in_specs=(
            P(("row", "col", "layer"), None, None, None),
            P(("row", "col", "layer")),
            P(("row", "col", "layer"), None),
        ),
        out_specs=P(("row", "layer"), "col", None, None),
        check_vma=False,
    )
```

profile of v0, /device:TPU:0, one launch (start us, length us, event | category | flops | bytes accessed | tf_op | source)
XLA Modules:
  0.0 2838.5 jit_solution(2040272807180117148)
XLA Ops:
  15.2 14.1 copy.39
  35.6 296.6 %all-to-all-done.4 = bf16[16,16,2,128,128]{4,3,2,0,1:T(8,128)(2,1)} async-done(((bf16[16,16,2,128,128]{4,3,2,0,1:T(8,128)(2,1)}), bf16[16,16,2,128,128]{4,3,2,0,1:T(8,128)(2,1)}, u32[]{:S(2)}, u32[]{:S(2)}) %all-to-all-start.4) | async-done | bytes 16777248 | tf_op jit(solution)/shard_map/all_to_all | solution.py:40
  337.7 42.9 %scatter_fusion = bf16[128,2,128,128]{3,2,1,0:T(8,128)(2,1)} fusion(bf16[128,2,128,128]{3,2,1,0:T(8,128)(2,1)} %broadcast_in_dim.81, s32[256]{0:T(256)S(1)} %bitcast.92, bf16[256,2,128,128]{3,2,1,0:T(8,128)(2,1)} %bitcast.21), kind=kCustom, calls=%fused_computation.4 | custom fusion | bytes 50332672 | tf_op jit(solution)/shard_map/scatter | solution.py:56
  380.6 18.7 all_to_all.95
  399.3 10.4 copy.40
  411.2 69.9 %all-to-all-start.1 = ((s32[16,16,2]{0,2,1:T(2,128)}), s32[16,16,2]{0,2,1:T(2,128)S(1)}, u32[]{:S(2)}, u32[]{:S(2)}) async-start(s32[16,16,2]{0,2,1:T(2,128)} %bitcast.2), calls=%async_computation.1 | async-start | bytes 32768 | tf_op jit(solution)/shard_map/all_to_all | solution.py:41
  493.1 16.8 all-gather
  522.3 151.9 %all-gather.5.cloned.1.call-done = bf16[128,4,128,128]{3,2,1,0:T(8,128)(2,1)} async-done(((bf16[64,4,128,128]{3,2,1,0:T(8,128)(2,1)}), bf16[128,4,128,128]{3,2,1,0:T(8,128)(2,1)}) %all-gather.5.cloned.1.call-update) | async-done | bytes 16777232 | tf_op jit(solution)/shard_map/all_gather | solution.py:68
  674.2 1268.5 %all-gather.7.cloned.1.call-done = bf16[128,16,128,128]{3,2,1,0:T(8,128)(2,1)} async-done(((bf16[128,2,128,128]{3,2,1,0:T(8,128)(2,1)}), bf16[128,16,128,128]{3,2,1,0:T(8,128)(2,1)}) %all-gather.7.cloned.1.call-update) | async-done | bytes 67108880 | tf_op jit(solution)/shard_map/all_gather | solution.py:76
  1942.7 835.0 %while.12 = (s32[]{:T(128)}, f32[16,8,4,128,128]{4,3,2,1,0:T(8,128)}, s32[16]{0:T(128)S(1)}, s32[128,16]{1,0:T(8,128)S(1)}, s32[16,8,4]{2,1,0:T(8,128)S(1)}, /*i...) while((s32[]{:T(128)}, ...), condition=%wide.region_4.5_spmd.clone, body=%wide.region_3.4_spmd.clone.sunk | while | flops 2155873536 | bytes 98579704 | solution.py:94
  1945.2 14.4 gather_fusion
  1959.6 21.6 copy.57
  1997.3 14.4 gather_fusion
  2011.7 21.6 copy.57
  2049.6 14.4 gather_fusion
  2064.0 21.6 copy.57
  2085.5 10.3 fusion.38
  2101.8 14.4 gather_fusion
  2116.2 21.6 copy.57
  2153.9 14.4 gather_fusion
  2168.3 21.6 copy.57
  2189.9 10.3 fusion.38
  2206.1 14.4 gather_fusion
  2220.5 21.6 copy.57
  2258.4 14.4 gather_fusion
  2272.8 21.6 copy.57
  2310.6 14.5 gather_fusion
  2325.0 21.6 copy.57
  2346.6 10.3 fusion.38
  2362.8 14.4 gather_fusion
  2377.2 21.6 copy.57
  2415.0 14.4 gather_fusion
  2429.3 21.6 copy.57
  2450.9 10.3 fusion.38
  2467.2 14.4 gather_fusion
  2481.6 21.6 copy.57
  2519.3 14.4 gather_fusion
  2533.7 21.6 copy.57
  2571.5 14.4 gather_fusion
  2585.9 21.6 copy.57
  2607.5 10.3 fusion.38
  2623.7 14.3 gather_fusion
  2638.0 21.6 copy.57
  2675.8 14.3 gather_fusion
  2690.2 21.6 copy.57
  2728.0 14.4 gather_fusion
  2742.4 21.6 copy.57
  2777.7 45.1 %reduce-scatter.2.cloned.1.call-done = f32[64,4,128,128]{3,2,1,0:T(8,128)} async-done(((f32[128,4,128,128]{3,2,1,0:T(8,128)}), f32[64,4,128,128]{3,2,1,0:T(8,128)}) %reduce-scatter.2.cloned.1.call-update) | async-done | bytes 16777232 | tf_op jit(solution)/shard_map/reduce_scatter | solution.py:96
  (214 shorter events, 252.0 us)
Async XLA Ops:
  7.8 21.5 all-to-all-start
  29.3 302.8 %all-to-all-start.4 = ((bf16[16,16,2,128,128]{4,3,2,0,1:T(8,128)(2,1)}), bf16[16,16,2,128,128]{4,3,2,0,1:T(8,128)(2,1)}, u32[]{:S(2)}, u32[]{:S(2)}) async-start(bf16[16,16,2,128,128]{4,3,2,0,1:T(8,128)(2,1)} %copy.39), calls=%async_computation.4 | async-start | bytes 33554432 | tf_op jit(solution)/shard_map/all_to_all | solution.py:40
  35.4 638.8 %all-gather.5.cloned.1.call-start = ((), (), s32[]{:S(2)}) async-start(), calls=%async_computation.7 | async-start | bytes 25165824 | tf_op jit(solution)/shard_map/all_gather | solution.py:68
  399.3 11.2 copy-start
  409.8 1532.9 %all-gather.7.cloned.1.call-start = ((), (), s32[]{:S(2)}) async-start(), calls=%async_computation.8 | async-start | bytes 75497472 | tf_op jit(solution)/shard_map/all_gather | solution.py:76
  411.2 76.4 %all-to-all-start.1 = ((s32[16,16,2]{0,2,1:T(2,128)}), s32[16,16,2]{0,2,1:T(2,128)S(1)}, u32[]{:S(2)}, u32[]{:S(2)}) async-start(s32[16,16,2]{0,2,1:T(2,128)} %bitcast.2), calls=%async_computation.1 | async-start | bytes 32768 | tf_op jit(solution)/shard_map/all_to_all | solution.py:41
  489.8 20.1 all-to-all-start.2
  509.9 10.1 all-to-all-start.3
  513.4 2309.4 %reduce-scatter.2.cloned.1.call-start = ((), (), s32[]{:S(2)}) async-start(), calls=%async_computation.9 | async-start | bytes 50331648 | tf_op jit(solution)/shard_map/reduce_scatter | solution.py:96
Sparse Core Ops, SparseCore 0:
  409.9 264.2 all-gather.4
  675.7 1266.9 all-gather.6
  2777.8 44.9 reduce-scatter.1
where the time goes:
time: 2850 us; the launch traced here: 2840 us
  waiting for transfers between devices  1770 us (62%)
  local copies, waits for them, and re-layouts  738 us (26%)
  matrix products  165 us (6%)
  starting transfers between devices  90.2 us (3%)
  blocking collectives  39.9 us (1%)
    all_gather x1, waiting for transfers between devices, shards(): piece_blocks = lax.all_gather(row_tile, 'col', axis=1, tiled=True)  1270 us
    gather x32, local copies, waits for them, and re-layouts, one_block(): chosen = column_table[panel_steps[None, :], row_offsets]  575 us
    all_to_all x1, waiting for transfers between devices, shards(): lax.all_to_all(outgoing[0], ('col', 'layer'), split_axis=1, concat_axis=0...  297 us
    dot_general x16, matrix products, one_block(): jnp.einsum('mtab,mtsbc->msac', left_blocks, chosen, preferred_element_typ...  165 us
    all_gather x1, waiting for transfers between devices, shards(): lax.all_gather(column_tile, 'row', axis=0, tiled=True)  152 us
    all_to_all x1, starting transfers between devices, shards(): lax.all_to_all(outgoing[1], ('col', 'layer'), split_axis=1, concat_axis=0...  69.9 us
  transfers between devices with their start and end apart: 8, of which 6 were waited for; matrix products, arithmetic and copies ran while one was open for 1% of the time, Pallas kernels for 0%

commit v1 on v0

--- a/solution.py
+++ b/solution.py
@@ -4,6 +4,24 @@
 from jax.sharding import PartitionSpec as P
 
 NB = 256
+
+
+def ring_gather(shard, axis, dim):
+    ways, here, step = (lax.axis_size(axis), lax.axis_index(axis), shard.shape[dim])
+    shape = [n * ways if d == dim else n for d, n in enumerate(shard.shape)]
+    full = lax.dynamic_update_slice_in_dim(
+        jnp.zeros(shape, shard.dtype), shard, here * step, axis=dim
+    )
+    going_up = going_down = shard
+    for far in range(1, ways // 2 + 1):
+        going_up = lax.ppermute(going_up, axis, [(d, (d + 1) % ways) for d in range(ways)])
+        full = lax.dynamic_update_slice_in_dim(full, going_up, (here - far) % ways * step, axis=dim)
+        if 2 * far < ways:
+            going_down = lax.ppermute(going_down, axis, [(d, (d - 1) % ways) for d in range(ways)])
+            full = lax.dynamic_update_slice_in_dim(
+                full, going_down, (here + far) % ways * step, axis=dim
+            )
+    return full
 
 
 def grid_positions(row_ids, panels, panel_width, grid_row, rows_grid, layers, per_device):
@@ -73,7 +91,7 @@
     )
     column_ids = column_ids.reshape(panels // layers, panel_width, slots_here)
     initial = jnp.zeros((tile_rows, slots_here, block_size, block_size), jnp.float32)
-    piece_blocks = lax.all_gather(row_tile, "col", axis=1, tiled=True)
+    piece_blocks = ring_gather(row_tile, "col", 1)
     piece_cols = lax.all_gather(col_tile, "col", axis=1, tiled=True)
     panel_count = piece_blocks.shape[1]
     panel_steps = jnp.arange(panel_count, dtype=jnp.int32)

time: 2850 us -> 2770 us (0.972)
  waiting for transfers between devices: 1770 us -> 1480 us
  local copies, waits for them, and re-layouts: 738 us -> 849 us
  starting transfers between devices: 90.2 us -> 182 us
    all_gather x1 -> x0, waiting for transfers between devices: 1270 us -> none  [shards(): piece_blocks = lax.all_gather(row_tile, 'col', axis=1, tiled=True)]
    ppermute x0 -> x7, waiting for transfers between devices: none -> 965 us  [the longest x4 914 us: ring_gather(): lax.ppermute(going_up, axis, [(d, (d + 1) % ways) for d in range(ways)])]
    all_to_all x1, waiting for transfers between devices: 5.75 us -> 175 us  [shards(): lax.all_to_all(outgoing[1], ('col', 'layer'), split_axis=1, concat_axis=0...]
    all_gather x1, waiting for transfers between devices: 152 us -> 0.01 us  [shards(): lax.all_gather(column_tile, 'row', axis=0, tiled=True)]
    ppermute x0 -> x7, starting transfers between devices: none -> 116 us  [the longest x3 85.4 us: ring_gather(): lax.ppermute(going_down, axis, [(d, (d - 1) % ways) for d in range(ways)])]
    dynamic_update_slice x0 -> x8, local copies, waits for them, and re-layouts: none -> 82.7 us  [the longest x4 41.4 us: ring_gather(): lax.dynamic_update_slice_in_dim(full, going_up, (here - far) % ways * ste...]
  transfers between devices with their start and end apart: 8 -> 14, of which waited for: 6 -> 9; matrix products, arithmetic and copies ran while one was open for 1% -> 5% of each run, Pallas kernels for 0% -> 0%
where the time goes in v1:
time: 2770 us; the launch traced here: 2760 us
  waiting for transfers between devices  1480 us (53%)
  local copies, waits for them, and re-layouts  849 us (31%)
  starting transfers between devices  182 us (7%)
  matrix products  165 us (6%)
  blocking collectives  41.2 us (1%)
    ppermute x4, waiting for transfers between devices, ring_gather(): lax.ppermute(going_up, axis, [(d, (d + 1) % ways) for d in range(ways)])  914 us
    gather x32, local copies, waits for them, and re-layouts, one_block(): chosen = column_table[panel_steps[None, :], row_offsets]  576 us
    all_to_all x1, waiting for transfers between devices, shards(): lax.all_to_all(outgoing[0], ('col', 'layer'), split_axis=1, concat_axis=0...  297 us
    all_to_all x1, waiting for transfers between devices, shards(): lax.all_to_all(outgoing[1], ('col', 'layer'), split_axis=1, concat_axis=0...  175 us
    dot_general x16, matrix products, one_block(): jnp.einsum('mtab,mtsbc->msac', left_blocks, chosen, preferred_element_typ...  165 us
    ppermute x3, starting transfers between devices, ring_gather(): lax.ppermute(going_down, axis, [(d, (d - 1) % ways) for d in range(ways)])  85.4 us
  transfers between devices with their start and end apart: 14, of which 9 were waited for; matrix products, arithmetic and copies ran while one was open for 5% of the time, Pallas kernels for 0%

profile of v1, /device:TPU:0, one launch (start us, length us, event | category | flops | bytes accessed | tf_op | source)
XLA Modules:
  0.0 2757.4 jit_solution(17503473593993878914)
XLA Ops:
  35.6 296.6 %all-to-all-done.4 = bf16[16,16,2,128,128]{4,3,2,0,1:T(8,128)(2,1)} async-done(((bf16[16,16,2,128,128]{4,3,2,0,1:T(8,128)(2,1)}), bf16[16,16,2,128,128]{4,3,2,0,1:T(8,128)(2,1)}, u32[]{:S(2)}, u32[]{:S(2)}) %all-to-all-start.4) | async-done | bytes 16777248 | tf_op jit(solution)/shard_map/all_to_all | solution.py:58
  337.6 46.1 %scatter_fusion = bf16[128,2,128,128]{3,2,1,0:T(8,128)(2,1)} fusion(bf16[128,2,128,128]{3,2,1,0:T(8,128)(2,1)} %broadcast_in_dim.84, s32[256]{0:T(256)S(1)} %bitcast.92, bf16[256,2,128,128]{3,2,1,0:T(8,128)(2,1)} %bitcast.21), kind=kCustom, calls=%fused_computation.4 | custom fusion | bytes 50332672 | tf_op jit(solution)/shard_map/scatter | solution.py:74
  383.7 23.0 collective-permute-start
  406.8 45.8 %collective-permute-start.1 = (bf16[128,2,128,128]{3,2,1,0:T(8,128)(2,1)}, bf16[128,2,128,128]{3,2,1,0:T(8,128)(2,1)}, u32[]{:S(2)}, u32[]{:S(2)}) collective-permute-start(bf16[128,2,128,128]{3,2,1,0:T(8,128)(2,1)} %scatter_fusion), channel_id=1, source_target_pairs={{0,14},{2,0},{4,2},{6,4},{8,6},{10,8},{12,10},{14,12},{1,15},{3,1}... | collective-permute-start | bytes 25165832 | tf_op jit(solution)/shard_map/ppermute | solution.py:20
  452.5 314.9 %collective-permute-done = bf16[128,2,128,128]{3,2,1,0:T(8,128)(2,1)S(1)} collective-permute-done((bf16[128,2,128,128]{3,2,1,0:T(8,128)(2,1)}, bf16[128,2,128,128]{3,2,1,0:T(8,128)(2,1)S(1)}, u32[]{:S(2)}, u32[]{:S(2)}) %collective-permute-start) | collective-permute-done | bytes 8388640 | tf_op jit(solution)/shard_map/ppermute | solution.py:17
  773.1 37.8 %collective-permute-done.1 = bf16[128,2,128,128]{3,2,1,0:T(8,128)(2,1)} collective-permute-done((bf16[128,2,128,128]{3,2,1,0:T(8,128)(2,1)}, bf16[128,2,128,128]{3,2,1,0:T(8,128)(2,1)}, u32[]{:S(2)}, u32[]{:S(2)}) %collective-permute-start.1) | collective-permute-done | bytes 8388640 | tf_op jit(solution)/shard_map/ppermute | solution.py:20
  818.4 314.2 %collective-permute-done.2 = bf16[128,2,128,128]{3,2,1,0:T(8,128)(2,1)} collective-permute-done((bf16[128,2,128,128]{3,2,1,0:T(8,128)(2,1)S(1)}, bf16[128,2,128,128]{3,2,1,0:T(8,128)(2,1)}, u32[]{:S(2)}, u32[]{:S(2)}) %collective-permute-start.2) | collective-permute-done | bytes 8388640 | tf_op jit(solution)/shard_map/ppermute | solution.py:17
  1135.2 18.5 all_to_all.95
  1177.1 32.0 %collective-permute-start.5 = (bf16[128,2,128,128]{3,2,1,0:T(8,128)(2,1)}, bf16[128,2,128,128]{3,2,1,0:T(8,128)(2,1)}, u32[]{:S(2)}, u32[]{:S(2)}) collective-permute-start(bf16[128,2,128,128]{3,2,1,0:T(8,128)(2,1)} %collective-permute-done.3), channel_id=1, source_target_pairs={{0,14},{2,0},{4,2},{6,4},{8,6},{10,8},{12,10},{14,12},{1,15},{3,1}... | collective-permute-start | bytes 25165832 | tf_op jit(solution)/shard_map/ppermute | solution.py:20
  1209.1 285.1 %collective-permute-done.4 = bf16[128,2,128,128]{3,2,1,0:T(8,128)(2,1)} collective-permute-done((bf16[128,2,128,128]{3,2,1,0:T(8,128)(2,1)}, bf16[128,2,128,128]{3,2,1,0:T(8,128)(2,1)}, u32[]{:S(2)}, u32[]{:S(2)}) %collective-permute-start.4) | collective-permute-done | bytes 8388640 | tf_op jit(solution)/shard_map/ppermute | solution.py:17
  1497.4 46.4 %all-to-all-start.1 = ((s32[16,16,2]{0,2,1:T(2,128)}), s32[16,16,2]{0,2,1:T(2,128)S(1)}, u32[]{:S(2)}, u32[]{:S(2)}) async-start(s32[16,16,2]{0,2,1:T(2,128)} %bitcast.2), calls=%async_computation.1 | async-start | bytes 32768 | tf_op jit(solution)/shard_map/all_to_all | solution.py:59
  1544.6 175.3 %all-to-all-done.1 = s32[16,16,2]{0,2,1:T(2,128)S(1)} async-done(((s32[16,16,2]{0,2,1:T(2,128)}), s32[16,16,2]{0,2,1:T(2,128)S(1)}, u32[]{:S(2)}, u32[]{:S(2)}) %all-to-all-start.1) | async-done | bytes 2080 | tf_op jit(solution)/shard_map/all_to_all | solution.py:59
  1725.2 18.3 all-gather
  1755.7 21.3 broadcast_in_dim.85
  1859.7 835.9 %while.12 = (s32[]{:T(128)}, f32[16,8,4,128,128]{4,3,2,1,0:T(8,128)}, s32[16]{0:T(128)S(1)}, s32[128,16]{1,0:T(8,128)S(1)}, s32[16,8,4]{2,1,0:T(8,128)S(1)}, /*i...) while((s32[]{:T(128)}, ...), condition=%wide.region_4.5_spmd.clone, body=%wide.region_3.4_spmd.clone.sunk | while | flops 2155873536 | bytes 98579704 | solution.py:112
  1862.2 14.4 gather_fusion
  1876.6 21.6 copy.57
  1914.5 14.4 gather_fusion
  1928.9 21.6 copy.57
  1966.7 14.4 gather_fusion
  1981.2 21.6 copy.57
  2019.0 14.4 gather_fusion
  2033.4 21.6 copy.57
  2071.2 14.4 gather_fusion
  2085.7 21.6 copy.57
  2123.5 14.4 gather_fusion
  2137.9 21.6 copy.57
  2175.8 14.4 gather_fusion
  2190.2 21.6 copy.57
  2228.1 14.5 gather_fusion
  2242.6 21.6 copy.57
  2280.3 14.4 gather_fusion
  2294.8 21.6 copy.57
  2332.6 14.4 gather_fusion
  2347.0 21.6 copy.57
  2384.8 14.4 gather_fusion
  2399.2 21.6 copy.57
  2437.1 14.4 gather_fusion
  2451.5 21.6 copy.57
  2489.3 14.4 gather_fusion
  2503.7 21.6 copy.57
  2541.5 14.4 gather_fusion
  2555.9 21.6 copy.57
  2593.7 14.4 gather_fusion
  2608.1 21.6 copy.57
  2646.0 14.4 gather_fusion
  2660.4 21.6 copy.57
  2695.7 45.7 %reduce-scatter.2.cloned.1.call-done = f32[64,4,128,128]{3,2,1,0:T(8,128)} async-done(((f32[128,4,128,128]{3,2,1,0:T(8,128)}), f32[64,4,128,128]{3,2,1,0:T(8,128)}) %reduce-scatter.2.cloned.1.call-update) | async-done | bytes 16777232 | tf_op jit(solution)/shard_map/reduce_scatter | solution.py:114
  (236 shorter events, 435.5 us)
Async XLA Ops:
  7.8 21.5 all-to-all-start
  29.3 302.8 %all-to-all-start.4 = ((bf16[16,16,2,128,128]{4,3,2,0,1:T(8,128)(2,1)}), bf16[16,16,2,128,128]{4,3,2,0,1:T(8,128)(2,1)}, u32[]{:S(2)}, u32[]{:S(2)}) async-start(bf16[16,16,2,128,128]{4,3,2,0,1:T(8,128)(2,1)} %copy.39), calls=%async_computation.4 | async-start | bytes 33554432 | tf_op jit(solution)/shard_map/all_to_all | solution.py:58
  35.3 1824.4 %all-gather.4.cloned.1.call-start = ((), (), s32[]{:S(2)}) async-start(), calls=%async_computation.7 | async-start | bytes 25165824 | tf_op jit(solution)/shard_map/all_gather | solution.py:86
  383.7 383.8 %collective-permute-start = (bf16[128,2,128,128]{3,2,1,0:T(8,128)(2,1)}, bf16[128,2,128,128]{3,2,1,0:T(8,128)(2,1)S(1)}, u32[]{:S(2)}, u32[]{:S(2)}) collective-permute-start(bf16[128,2,128,128]{3,2,1,0:T(8,128)(2,1)} %scatter_fusion), channel_id=1, source_target_pairs={{0,2},{2,4},{4,6},{6,8},{8,10},{10,12},{12,14},{14,0},{1,3},{3,5},... | collective-permute-start | bytes 25165832 | tf_op jit(solution)/shard_map/ppermute | solution.py:17
  406.8 404.1 %collective-permute-start.1 = (bf16[128,2,128,128]{3,2,1,0:T(8,128)(2,1)}, bf16[128,2,128,128]{3,2,1,0:T(8,128)(2,1)}, u32[]{:S(2)}, u32[]{:S(2)}) collective-permute-start(bf16[128,2,128,128]{3,2,1,0:T(8,128)(2,1)} %scatter_fusion), channel_id=1, source_target_pairs={{0,14},{2,0},{4,2},{6,4},{8,6},{10,8},{12,10},{14,12},{1,15},{3,1}... | collective-permute-start | bytes 25165832 | tf_op jit(solution)/shard_map/ppermute | solution.py:20
  767.5 3.2 copy-start
  770.7 361.9 %collective-permute-start.2 = (bf16[128,2,128,128]{3,2,1,0:T(8,128)(2,1)S(1)}, bf16[128,2,128,128]{3,2,1,0:T(8,128)(2,1)}, u32[]{:S(2)}, u32[]{:S(2)}) collective-permute-start(bf16[128,2,128,128]{3,2,1,0:T(8,128)(2,1)S(1)} %collective-permute-done), channel_id=1, source_target_pairs={{0,2},{2,4},{4,6},{6,8},{8,10},{10,12},{12,14},{14,0},{1,3},{3,5},... | collective-permute-start | bytes 25165832 | tf_op jit(solution)/shard_map/ppermute | solution.py:17
  810.9 366.3 %collective-permute-start.3 = (bf16[128,2,128,128]{3,2,1,0:T(8,128)(2,1)}, bf16[128,2,128,128]{3,2,1,0:T(8,128)(2,1)}, u32[]{:S(2)}, u32[]{:S(2)}) collective-permute-start(bf16[128,2,128,128]{3,2,1,0:T(8,128)(2,1)} %collective-permute-done.1), channel_id=1, source_target_pairs={{0,14},{2,0},{4,2},{6,4},{8,6},{10,8},{12,10},{14,12},{1,15},{3,1}... | collective-permute-start | bytes 25165832 | tf_op jit(solution)/shard_map/ppermute | solution.py:20
  1132.6 361.6 %collective-permute-start.4 = (bf16[128,2,128,128]{3,2,1,0:T(8,128)(2,1)}, bf16[128,2,128,128]{3,2,1,0:T(8,128)(2,1)}, u32[]{:S(2)}, u32[]{:S(2)}) collective-permute-start(bf16[128,2,128,128]{3,2,1,0:T(8,128)(2,1)} %collective-permute-done.2), channel_id=1, source_target_pairs={{0,2},{2,4},{4,6},{6,8},{8,10},{10,12},{12,14},{14,0},{1,3},{3,5},... | collective-permute-start | bytes 25165832 | tf_op jit(solution)/shard_map/ppermute | solution.py:17
  1153.7 343.0 %copy-start.1 = (s32[16,32]{1,0:T(8,128)S(1)}, s32[16,32]{1,0:T(8,128)}, u32[]{:S(2)}) copy-start(s32[16,32]{1,0:T(8,128)} %param.7) | copy-start | bytes 6148
  1177.1 662.0 %collective-permute-start.5 = (bf16[128,2,128,128]{3,2,1,0:T(8,128)(2,1)}, bf16[128,2,128,128]{3,2,1,0:T(8,128)(2,1)}, u32[]{:S(2)}, u32[]{:S(2)}) collective-permute-start(bf16[128,2,128,128]{3,2,1,0:T(8,128)(2,1)} %collective-permute-done.3), channel_id=1, source_target_pairs={{0,14},{2,0},{4,2},{6,4},{8,6},{10,8},{12,10},{14,12},{1,15},{3,1}... | collective-permute-start | bytes 25165832 | tf_op jit(solution)/shard_map/ppermute | solution.py:20
  1494.2 355.2 %collective-permute-start.6 = (bf16[128,2,128,128]{3,2,1,0:T(8,128)(2,1)}, bf16[128,2,128,128]{3,2,1,0:T(8,128)(2,1)}, u32[]{:S(2)}, u32[]{:S(2)}) collective-permute-start(bf16[128,2,128,128]{3,2,1,0:T(8,128)(2,1)} %collective-permute-done.4), channel_id=1, source_target_pairs={{0,2},{2,4},{4,6},{6,8},{8,10},{10,12},{12,14},{14,0},{1,3},{3,5},... | collective-permute-start | bytes 25165832 | tf_op jit(solution)/shard_map/ppermute | solution.py:17
  1497.4 222.5 %all-to-all-start.1 = ((s32[16,16,2]{0,2,1:T(2,128)}), s32[16,16,2]{0,2,1:T(2,128)S(1)}, u32[]{:S(2)}, u32[]{:S(2)}) async-start(s32[16,16,2]{0,2,1:T(2,128)} %bitcast.2), calls=%async_computation.1 | async-start | bytes 32768 | tf_op jit(solution)/shard_map/all_to_all | solution.py:59
  1722.0 21.6 all-to-all-start.2
  1743.6 10.1 all-to-all-start.3
  1747.1 994.3 %reduce-scatter.2.cloned.1.call-start = ((), (), s32[]{:S(2)}) async-start(), calls=%async_computation.8 | async-start | bytes 50331648 | tf_op jit(solution)/shard_map/reduce_scatter | solution.py:114
Sparse Core Ops, SparseCore 0:
  1164.3 240.9 all-gather.3
  2695.8 45.5 reduce-scatter.1
